TPU v7x, 512 devices: a whole 4x8x8 slice. The times are simulated.
512 devices in a mesh: rows: 64 (over x, y, core), vec: 8 (over z).
Axes of the slice: x: 4, y: 8, z: 8, core: 2. Of those that a mesh axis runs over, the one named last changes fastest.
Arguments:
- vectors: float32 [64, 131072], P('vec', 'rows'), may hold values from -6 to 6
- damage: float32 [131072], P('rows')
- diag_blocks: bfloat16 [1024, 128, 128], P('rows')
- upper_blocks: bfloat16 [8192, 128, 128], P('rows'), may hold values from -0.5 to 0.5
- block_rows: int32 [8192], P('rows'), may hold values from 0 to 1023, as said below
- block_cols: int32 [8192], P('rows'), may hold values from 1 to 1023, as said below
- live_slots: int32 [64], P('rows'), may hold values from 64 to 128, as said below
Outputs:
- product: float32 [64, 131072], P('vec', 'rows')
- projected: float32 [64, 64], P('vec')
Inputs may be any that keep to these rules, and one draw needn't show every extreme that they name: `block_rows`: the slots of device d name block rows d * 16 to (d + 1) * 16 - 1; a slot whose column lies on another device names one of the last 6 of these. block_cols[s] is greater than block_rows[s], and block_cols[s] // 16 lies between d and d + 3 for a slot of device d; some slots reach d + 3. A column on device e other than d is one of the first 6 block rows of e. A pair may appear in several slots; their blocks add. `live_slots`: some device has all its slots stored.
All inputs are finite; a program needn't handle non-finite values.
Results may differ from a plain program's by a relative error of at most 0.0029.
Values may be sent and summed in bfloat16 or wider, within the bound.
No kernel may reach another device: no remote copies, remote signals or barrier semaphores. Data moves between devices by JAX's collectives and lax.ppermute only.
A program may use at most 64 MiB of HBM per device.

v0:
```python
import jax
import jax.numpy as jnp
from jax import lax
from jax.sharding import PartitionSpec as P

REACH = 4
RIM = 6
resid_eta = 0.001


def passed_along(array, axis, by):
    devices = lax.axis_size(axis)
    pairs = [(i, i + by) for i in range(devices) if 0 <= i + by < devices]
    return lax.ppermute(array, axis, pairs)


def on_device(vectors, damage, diag_blocks, upper_blocks, block_rows, block_cols, live_slots):
    vec_here, width = vectors.shape
    rb_here = diag_blocks.shape[0]
    block_size = diag_blocks.shape[1]
    slot_count = upper_blocks.shape[0]
    mine = lax.axis_index("rows")
    soft = jnp.sqrt((1.0 - damage) ** 2 + resid_eta)
    scaled = (vectors * soft[None, :]).astype(jnp.bfloat16).reshape(vec_here, rb_here, block_size)
    stored = (jnp.arange(slot_count) < live_slots[0]).astype(jnp.float32)
    local_rows = block_rows - mine * rb_here
    row_pick = (local_rows[:, None] == jnp.arange(rb_here)[None, :]).astype(jnp.float32) * stored[
        :, None
    ]
    own_rows = jnp.einsum(
        "vrb,sr->vsb", scaled, row_pick.astype(jnp.bfloat16), preferred_element_type=jnp.float32
    ).astype(jnp.bfloat16)
    accum = jnp.einsum("vrj,rij->vri", scaled, diag_blocks, preferred_element_type=jnp.float32)
    backward = jnp.einsum(
        "vsi,sij->vsj", own_rows, upper_blocks, preferred_element_type=jnp.float32
    )
    pieces = [scaled]
    for step in range(1, REACH):
        pieces.append(passed_along(scaled[:, :RIM], "rows", -step))
    window = jnp.concatenate(pieces, axis=1)
    relative = block_cols - mine * rb_here
    dev_step = relative // rb_here
    within = relative - dev_step * rb_here
    col_index = jnp.where(dev_step == 0, within, rb_here + (dev_step - 1) * RIM + within)
    span = window.shape[1]
    col_pick = (col_index[:, None] == jnp.arange(span)[None, :]).astype(jnp.float32) * stored[
        :, None
    ]
    far_cols = jnp.einsum(
        "vcb,sc->vsb", window, col_pick.astype(jnp.bfloat16), preferred_element_type=jnp.float32
    ).astype(jnp.bfloat16)
    forward = jnp.einsum("vsj,sij->vsi", far_cols, upper_blocks, preferred_element_type=jnp.float32)
    gathered = jnp.einsum("vsi,sr->vri", forward, row_pick, precision=lax.Precision.HIGHEST)
    spread = jnp.einsum("vsj,sc->vcj", backward, col_pick, precision=lax.Precision.HIGHEST)
    gathered, spread = (gathered, spread)
    accum = accum + gathered + spread[:, :rb_here]
    for step in range(1, REACH):
        low = rb_here + (step - 1) * RIM
        arrived = passed_along(spread[:, low : low + RIM], "rows", step)
        accum = accum.at[:, :RIM].add(arrived)
    product = soft[None, :] * accum.reshape(vec_here, width)
    partial_gram = jnp.dot(
        vectors,
        lax.all_gather(product.astype(jnp.bfloat16), "vec", axis=0, tiled=True)
        .astype(jnp.float32)
        .T,
        precision=lax.Precision.HIGHEST,
        preferred_element_type=jnp.float32,
    )
    total_dof = width * lax.axis_size("rows")
    projected = lax.psum(partial_gram, "rows") / total_dof
    return (product, projected)


def solution(mesh):
    return jax.shard_map(
        on_device,
        mesh=mesh,
        in_specs=(
            P("vec", "rows"),
            P("rows"),
            P("rows", None, None),
            P("rows", None, None),
            P("rows"),
            P("rows"),
            P("rows"),
        ),
        out_specs=(P("vec", "rows"), P("vec", None)),
        check_vma=False,
    )
```

profile of v0, /device:TPU:1, one launch (start us, length us, event | category | flops | bytes accessed | tf_op | source)
XLA Modules:
  0.0 186.2 jit_solution(1229719728883084545)
XLA Ops:
  0.6 0.0 copy-start
  0.6 0.8 add_sqrt_fusion
  1.4 0.9 fusion.16
  2.3 1.3 collective-permute-start.2
  3.6 1.3 collective-permute-start.1
  4.9 8.8 %collective-permute-start = (bf16[8,6,128]{2,0,1:T(8,128)(2,1)S(1)}, bf16[8,6,128]{2,0,1:T(8,128)(2,1)S(1)}, u32[]{:S(2)}, u32[]{:S(2)}) collective-permute-start(bf16[8,6,128]{2,0,1:T(8,128)(2,1)S(1)} %slice.91), channel_id=1, source_target_pairs={{8,0},{16,8},{24,16},{32,24},{40,32},{48,40},{56,48},{64,56},{72,6... | collective-permute-start | bytes 36872 | tf_op jit(solution)/shard_map/ppermute | solution.py:14
  14.3 0.8 broadcast_subtract_fusion
  15.2 0.8 compare_select_fusion
  16.0 0.3 fusion.17
  16.3 3.4 %fusion.12 = f32[128,8,128]{2,1,0:T(8,128)S(1)} fusion(bf16[128,128,128]{2,1,0:T(8,128)(2,1)} %param.16, bf16[128,8,128]{2,0,1:T(8,128)(2,1)S(1)} %fusion.17), kind=kOutput, calls=%fused_computation.15 | convolution fusion | flops 33554432 | bytes 4980736 | tf_op jit(solution)/shard_map/vsi,sij->vsj/dot_general | solution.py:34
  19.7 0.5 fusion.2
  20.1 0.0 copy-start.2
  20.2 6.0 %collective-permute-start.5 = (f32[8,6,128]{2,0,1:T(8,128)S(1)}, f32[8,6,128]{2,0,1:T(8,128)S(1)}, u32[]{:S(2)}, u32[]{:S(2)}) collective-permute-start(f32[8,6,128]{2,0,1:T(8,128)S(1)} %get-tuple-element.40), channel_id=1, source_target_pairs={{0,24},{8,32},{16,40},{24,48},{32,56},{40,64},{48,72},{56,80},{64,... | collective-permute-start | bytes 73736 | tf_op jit(solution)/shard_map/ppermute | solution.py:14
  26.2 3.4 %collective-permute-start.4 = (f32[8,6,128]{2,0,1:T(8,128)S(1)}, f32[8,6,128]{2,0,1:T(8,128)S(1)}, u32[]{:S(2)}, u32[]{:S(2)}) collective-permute-start(f32[8,6,128]{2,0,1:T(8,128)S(1)} %get-tuple-element.41), channel_id=1, source_target_pairs={{0,16},{8,24},{16,32},{24,40},{32,48},{40,56},{48,64},{56,72},{64,... | collective-permute-start | bytes 73736 | tf_op jit(solution)/shard_map/ppermute | solution.py:14
  29.5 1.9 %collective-permute-start.3 = (f32[8,6,128]{2,0,1:T(8,128)S(1)}, f32[8,6,128]{2,0,1:T(8,128)S(1)}, u32[]{:S(2)}, u32[]{:S(2)}) collective-permute-start(f32[8,6,128]{2,0,1:T(8,128)S(1)} %get-tuple-element.42), channel_id=1, source_target_pairs={{0,8},{8,16},{16,24},{24,32},{32,40},{40,48},{48,56},{56,64},{64,7... | collective-permute-start | bytes 73736 | tf_op jit(solution)/shard_map/ppermute | solution.py:14
  31.5 0.3 fusion.14
  31.8 2.3 %fusion.9 = f32[128,8,128]{2,1,0:T(8,128)S(1)} fusion(bf16[128,128,128]{2,1,0:T(8,128)(2,1)S(1)} %copy-done.1, bf16[128,8,128]{2,0,1:T(8,128)(2,1)S(1)} %fusion.14), kind=kOutput, calls=%fused_computation.13 | convolution fusion | flops 33554432 | bytes 4980736 | tf_op jit(solution)/shard_map/vsj,sij->vsi/dot_general | solution.py:52
  34.0 0.4 fusion.4
  34.5 0.4 fusion.1
  34.9 0.6 fusion.39
  35.6 20.4 %all_gather.3 = bf16[64,2048]{1,0:T(8,128)(2,1)S(1)} all-gather(bf16[8,2048]{1,0:T(8,128)(2,1)S(1)} %get-tuple-element.38), channel_id=1, replica_groups=mesh['rows'=64,'vec'=8] {'vec'}, dimensions={0}, use_global_device_ids=true | all-gather | bytes 294912 | tf_op jit(solution)/shard_map/all_gather | solution.py:64
  56.0 0.3 convolution_bitcast_fusion
  56.3 129.3 %psum.7 = f32[8,64]{1,0:T(8,128)S(1)} all-reduce(f32[8,64]{1,0:T(8,128)S(1)} %convolution_bitcast_fusion), channel_id=1, replica_groups=mesh['rows'=64,'vec'=8] {'rows'}, use_global_device_ids=true, to_apply=%region_0.1 | all-reduce | flops 512 | bytes 4096 | tf_op jit(solution)/shard_map/psum | solution.py:71
  185.6 0.6 broadcast_multiply_fusion
  (19 shorter events, 0.1 us)
Async XLA Ops:
  0.6 33.8 %copy-start = (bf16[16,128,128]{2,1,0:T(8,128)(2,1)S(1)}, bf16[16,128,128]{2,1,0:T(8,128)(2,1)}, u32[]{:S(2)}) copy-start(bf16[16,128,128]{2,1,0:T(8,128)(2,1)} %param.15) | copy-start | bytes 1572868
  2.3 27.2 %collective-permute-start.2 = (bf16[8,6,128]{2,0,1:T(8,128)(2,1)S(1)}, bf16[8,6,128]{2,0,1:T(8,128)(2,1)S(1)}, u32[]{:S(2)}, u32[]{:S(2)}) collective-permute-start(bf16[8,6,128]{2,0,1:T(8,128)(2,1)S(1)} %slice.91), channel_id=1, source_target_pairs={{24,0},{32,8},{40,16},{48,24},{56,32},{64,40},{72,48},{80,56},{88,... | collective-permute-start | bytes 36872 | tf_op jit(solution)/shard_map/ppermute | solution.py:14
  3.6 27.9 %collective-permute-start.1 = (bf16[8,6,128]{2,0,1:T(8,128)(2,1)S(1)}, bf16[8,6,128]{2,0,1:T(8,128)(2,1)S(1)}, u32[]{:S(2)}, u32[]{:S(2)}) collective-permute-start(bf16[8,6,128]{2,0,1:T(8,128)(2,1)S(1)} %slice.91), channel_id=1, source_target_pairs={{16,0},{24,8},{32,16},{40,24},{48,32},{56,40},{64,48},{72,56},{80,... | collective-permute-start | bytes 36872 | tf_op jit(solution)/shard_map/ppermute | solution.py:14
  4.9 26.6 %collective-permute-start = (bf16[8,6,128]{2,0,1:T(8,128)(2,1)S(1)}, bf16[8,6,128]{2,0,1:T(8,128)(2,1)S(1)}, u32[]{:S(2)}, u32[]{:S(2)}) collective-permute-start(bf16[8,6,128]{2,0,1:T(8,128)(2,1)S(1)} %slice.91), channel_id=1, source_target_pairs={{8,0},{16,8},{24,16},{32,24},{40,32},{48,40},{56,48},{64,56},{72,6... | collective-permute-start | bytes 36872 | tf_op jit(solution)/shard_map/ppermute | solution.py:14
  14.3 17.4 %copy-start.1 = (bf16[128,128,128]{2,1,0:T(8,128)(2,1)S(1)}, bf16[128,128,128]{2,1,0:T(8,128)(2,1)}, u32[]{:S(2)}) copy-start(bf16[128,128,128]{2,1,0:T(8,128)(2,1)} %param.16) | copy-start | bytes 12582916
  20.1 35.9 %copy-start.2 = (f32[8,2048]{1,0:T(8,128)S(1)}, f32[8,2048]{1,0:T(8,128)}, u32[]{:S(2)}) copy-start(f32[8,2048]{1,0:T(8,128)} %param.13) | copy-start | bytes 196612
  20.2 14.7 %collective-permute-start.5 = (f32[8,6,128]{2,0,1:T(8,128)S(1)}, f32[8,6,128]{2,0,1:T(8,128)S(1)}, u32[]{:S(2)}, u32[]{:S(2)}) collective-permute-start(f32[8,6,128]{2,0,1:T(8,128)S(1)} %get-tuple-element.40), channel_id=1, source_target_pairs={{0,24},{8,32},{16,40},{24,48},{32,56},{40,64},{48,72},{56,80},{64,... | collective-permute-start | bytes 73736 | tf_op jit(solution)/shard_map/ppermute | solution.py:14
  26.2 8.7 %collective-permute-start.4 = (f32[8,6,128]{2,0,1:T(8,128)S(1)}, f32[8,6,128]{2,0,1:T(8,128)S(1)}, u32[]{:S(2)}, u32[]{:S(2)}) collective-permute-start(f32[8,6,128]{2,0,1:T(8,128)S(1)} %get-tuple-element.41), channel_id=1, source_target_pairs={{0,16},{8,24},{16,32},{24,40},{32,48},{40,56},{48,64},{56,72},{64,... | collective-permute-start | bytes 73736 | tf_op jit(solution)/shard_map/ppermute | solution.py:14
  29.5 5.3 %collective-permute-start.3 = (f32[8,6,128]{2,0,1:T(8,128)S(1)}, f32[8,6,128]{2,0,1:T(8,128)S(1)}, u32[]{:S(2)}, u32[]{:S(2)}) collective-permute-start(f32[8,6,128]{2,0,1:T(8,128)S(1)} %get-tuple-element.42), channel_id=1, source_target_pairs={{0,8},{8,16},{16,24},{24,32},{32,40},{40,48},{48,56},{56,64},{64,7... | collective-permute-start | bytes 73736 | tf_op jit(solution)/shard_map/ppermute | solution.py:14
where the time goes:
time: 187 us; the launch traced here: 186 us
  blocking collectives  150 us (80%)
  starting transfers between devices  22.6 us (12%)
  matrix products  7.72 us (4%)
  other arithmetic  4.55 us (2%)
    psum x1, blocking collectives, on_device(): projected = lax.psum(partial_gram, 'rows') / total_dof  129 us
    ppermute x6, starting transfers between devices, passed_along(): return lax.ppermute(array, axis, pairs)  22.6 us
    all_gather x1, blocking collectives, on_device(): lax.all_gather(product.astype(jnp.bfloat16), 'vec', axis=0, tiled=True)  20.4 us
  transfers between devices with their start and end apart: 6, of which 0 were waited for; matrix products, arithmetic and copies ran while one was open for 5% of the time, Pallas kernels for 0%

commit v1 on v0

--- a/solution.py
+++ b/solution.py
@@ -1,3 +1,4 @@
+import functools
 import jax
 import jax.numpy as jnp
 from jax import lax
@@ -6,6 +7,14 @@
 REACH = 4
 RIM = 6
 resid_eta = 0.001
+
+
+def fix_column(values, comm_axis):
+    kept_arr = lax.all_gather(values, axis_name=comm_axis)
+    return jnp.sum(kept_arr, 0)
+
+
+take_cycles_now = functools.partial(fix_column, comm_axis="rows")
 
 
 def passed_along(array, axis, by):
@@ -68,7 +77,7 @@
         preferred_element_type=jnp.float32,
     )
     total_dof = width * lax.axis_size("rows")
-    projected = lax.psum(partial_gram, "rows") / total_dof
+    projected = take_cycles_now(partial_gram) / total_dof
     return (product, projected)
 
 

time: 187 us -> 105 us (0.56)
  blocking collectives: 150 us -> 68.3 us
    psum x1 -> x0, blocking collectives: 129 us -> none  [on_device(): projected = lax.psum(partial_gram, 'rows') / total_dof]
    all_gather x0 -> x1, blocking collectives: none -> 47.9 us  [fix_column(): kept_arr = lax.all_gather(values, axis_name=comm_axis)]
  transfers between devices with their start and end apart: 6 -> 6, of which waited for: 0 -> 0; matrix products, arithmetic and copies ran while one was open for 5% -> 9% of each run, Pallas kernels for 0% -> 0%
where the time goes in v1:
time: 105 us
  blocking collectives  68.3 us (65%)
  starting transfers between devices  22.6 us (22%)
  matrix products  7.72 us (7%)
  other arithmetic  4.62 us (4%)
  between operations  1.52 us (1%)
    all_gather x1, blocking collectives, fix_column(): kept_arr = lax.all_gather(values, axis_name=comm_axis)  47.9 us
    ppermute x6, starting transfers between devices, passed_along(): return lax.ppermute(array, axis, pairs)  22.6 us
    all_gather x1, blocking collectives, on_device(): lax.all_gather(product.astype(jnp.bfloat16), 'vec', axis=0, tiled=True)  20.4 us
    dot_general x1, matrix products, on_device(): jnp.einsum('vsi,sij->vsj', own_rows, upper_blocks, preferred_element_type...  3.38 us
    dot_general x1, matrix products, on_device(): jnp.einsum('vsj,sij->vsi', far_cols, upper_blocks, preferred_element_type...  2.25 us
  transfers between devices with their start and end apart: 6, of which 0 were waited for; matrix products, arithmetic and copies ran while one was open for 9% of the time, Pallas kernels for 0%

profile of v1, /device:TPU:1, one launch (start us, length us, event | category | flops | bytes accessed | tf_op | source)
XLA Modules:
  0.0 104.9 jit_solution(13496637133949277237)
XLA Ops:
  0.6 0.0 copy-start
  0.6 0.8 add_sqrt_fusion
  1.4 0.9 fusion.16
  2.3 1.3 %collective-permute-start.2 = (bf16[8,6,128]{2,0,1:T(8,128)(2,1)S(1)}, bf16[8,6,128]{2,0,1:T(8,128)(2,1)S(1)}, u32[]{:S(2)}, u32[]{:S(2)}) collective-permute-start(bf16[8,6,128]{2,0,1:T(8,128)(2,1)S(1)} %slice.91), channel_id=1, source_target_pairs={{24,0},{32,8},{40,16},{48,24},{56,32},{64,40},{72,48},{80,56},{88,... | collective-permute-start | bytes 36872 | tf_op jit(solution)/shard_map/ppermute | solution.py:23
  3.6 1.3 %collective-permute-start.1 = (bf16[8,6,128]{2,0,1:T(8,128)(2,1)S(1)}, bf16[8,6,128]{2,0,1:T(8,128)(2,1)S(1)}, u32[]{:S(2)}, u32[]{:S(2)}) collective-permute-start(bf16[8,6,128]{2,0,1:T(8,128)(2,1)S(1)} %slice.91), channel_id=1, source_target_pairs={{16,0},{24,8},{32,16},{40,24},{48,32},{56,40},{64,48},{72,56},{80,... | collective-permute-start | bytes 36872 | tf_op jit(solution)/shard_map/ppermute | solution.py:23
  4.9 8.8 %collective-permute-start = (bf16[8,6,128]{2,0,1:T(8,128)(2,1)S(1)}, bf16[8,6,128]{2,0,1:T(8,128)(2,1)S(1)}, u32[]{:S(2)}, u32[]{:S(2)}) collective-permute-start(bf16[8,6,128]{2,0,1:T(8,128)(2,1)S(1)} %slice.91), channel_id=1, source_target_pairs={{8,0},{16,8},{24,16},{32,24},{40,32},{48,40},{56,48},{64,56},{72,6... | collective-permute-start | bytes 36872 | tf_op jit(solution)/shard_map/ppermute | solution.py:23
  14.3 0.8 broadcast_subtract_fusion
  15.2 0.8 compare_select_fusion
  16.0 0.3 fusion.17
  16.3 3.4 %fusion.12 = f32[128,8,128]{2,1,0:T(8,128)S(1)} fusion(bf16[128,128,128]{2,1,0:T(8,128)(2,1)} %param.16, bf16[128,8,128]{2,0,1:T(8,128)(2,1)S(1)} %fusion.17), kind=kOutput, calls=%fused_computation.15 | convolution fusion | flops 33554432 | bytes 4980736 | tf_op jit(solution)/shard_map/vsi,sij->vsj/dot_general | solution.py:43
  19.7 0.5 fusion.2
  20.2 6.0 %collective-permute-start.5 = (f32[8,6,128]{2,0,1:T(8,128)S(1)}, f32[8,6,128]{2,0,1:T(8,128)S(1)}, u32[]{:S(2)}, u32[]{:S(2)}) collective-permute-start(f32[8,6,128]{2,0,1:T(8,128)S(1)} %get-tuple-element.40), channel_id=1, source_target_pairs={{0,24},{8,32},{16,40},{24,48},{32,56},{40,64},{48,72},{56,80},{64,... | collective-permute-start | bytes 73736 | tf_op jit(solution)/shard_map/ppermute | solution.py:23
  26.2 3.4 %collective-permute-start.4 = (f32[8,6,128]{2,0,1:T(8,128)S(1)}, f32[8,6,128]{2,0,1:T(8,128)S(1)}, u32[]{:S(2)}, u32[]{:S(2)}) collective-permute-start(f32[8,6,128]{2,0,1:T(8,128)S(1)} %get-tuple-element.41), channel_id=1, source_target_pairs={{0,16},{8,24},{16,32},{24,40},{32,48},{40,56},{48,64},{56,72},{64,... | collective-permute-start | bytes 73736 | tf_op jit(solution)/shard_map/ppermute | solution.py:23
  29.5 1.9 %collective-permute-start.3 = (f32[8,6,128]{2,0,1:T(8,128)S(1)}, f32[8,6,128]{2,0,1:T(8,128)S(1)}, u32[]{:S(2)}, u32[]{:S(2)}) collective-permute-start(f32[8,6,128]{2,0,1:T(8,128)S(1)} %get-tuple-element.42), channel_id=1, source_target_pairs={{0,8},{8,16},{16,24},{24,32},{32,40},{40,48},{48,56},{56,64},{64,7... | collective-permute-start | bytes 73736 | tf_op jit(solution)/shard_map/ppermute | solution.py:23
  31.5 0.3 fusion.14
  31.8 2.3 %fusion.9 = f32[128,8,128]{2,1,0:T(8,128)S(1)} fusion(bf16[128,128,128]{2,1,0:T(8,128)(2,1)S(1)} %copy-done.1, bf16[128,8,128]{2,0,1:T(8,128)(2,1)S(1)} %fusion.14), kind=kOutput, calls=%fused_computation.13 | convolution fusion | flops 33554432 | bytes 4980736 | tf_op jit(solution)/shard_map/vsj,sij->vsi/dot_general | solution.py:61
  34.0 0.4 fusion.4
  34.5 0.4 fusion.1
  34.9 0.6 fusion.39
  35.6 20.4 %all_gather.9 = bf16[64,2048]{1,0:T(8,128)(2,1)S(1)} all-gather(bf16[8,2048]{1,0:T(8,128)(2,1)S(1)} %get-tuple-element.38), channel_id=1, replica_groups=mesh['rows'=64,'vec'=8] {'vec'}, dimensions={0}, use_global_device_ids=true | all-gather | bytes 294912 | tf_op jit(solution)/shard_map/all_gather | solution.py:73
  56.0 0.3 convolution_bitcast_fusion
  56.3 47.9 %all-gather = f32[512,64]{1,0:T(8,128)S(1)} all-gather(f32[8,64]{1,0:T(8,128)S(1)} %convolution_bitcast_fusion), channel_id=2, replica_groups=mesh['rows'=64,'vec'=8] {'rows'}, dimensions={0}, use_global_device_ids=true | all-gather | bytes 133120 | tf_op jit(solution)/shard_map/all_gather | solution.py:13
  104.2 0.1 bitcast_reduce_fusion
  104.3 0.6 broadcast_multiply_fusion
  (20 shorter events, 0.1 us)
Async XLA Ops:
  0.6 33.8 %copy-start = (bf16[16,128,128]{2,1,0:T(8,128)(2,1)S(1)}, bf16[16,128,128]{2,1,0:T(8,128)(2,1)}, u32[]{:S(2)}) copy-start(bf16[16,128,128]{2,1,0:T(8,128)(2,1)} %param.15) | copy-start | bytes 1572868
  2.3 27.2 %collective-permute-start.2 = (bf16[8,6,128]{2,0,1:T(8,128)(2,1)S(1)}, bf16[8,6,128]{2,0,1:T(8,128)(2,1)S(1)}, u32[]{:S(2)}, u32[]{:S(2)}) collective-permute-start(bf16[8,6,128]{2,0,1:T(8,128)(2,1)S(1)} %slice.91), channel_id=1, source_target_pairs={{24,0},{32,8},{40,16},{48,24},{56,32},{64,40},{72,48},{80,56},{88,... | collective-permute-start | bytes 36872 | tf_op jit(solution)/shard_map/ppermute | solution.py:23
  3.6 27.9 %collective-permute-start.1 = (bf16[8,6,128]{2,0,1:T(8,128)(2,1)S(1)}, bf16[8,6,128]{2,0,1:T(8,128)(2,1)S(1)}, u32[]{:S(2)}, u32[]{:S(2)}) collective-permute-start(bf16[8,6,128]{2,0,1:T(8,128)(2,1)S(1)} %slice.91), channel_id=1, source_target_pairs={{16,0},{24,8},{32,16},{40,24},{48,32},{56,40},{64,48},{72,56},{80,... | collective-permute-start | bytes 36872 | tf_op jit(solution)/shard_map/ppermute | solution.py:23
  4.9 26.6 %collective-permute-start = (bf16[8,6,128]{2,0,1:T(8,128)(2,1)S(1)}, bf16[8,6,128]{2,0,1:T(8,128)(2,1)S(1)}, u32[]{:S(2)}, u32[]{:S(2)}) collective-permute-start(bf16[8,6,128]{2,0,1:T(8,128)(2,1)S(1)} %slice.91), channel_id=1, source_target_pairs={{8,0},{16,8},{24,16},{32,24},{40,32},{48,40},{56,48},{64,56},{72,6... | collective-permute-start | bytes 36872 | tf_op jit(solution)/shard_map/ppermute | solution.py:23
  14.3 17.4 %copy-start.1 = (bf16[128,128,128]{2,1,0:T(8,128)(2,1)S(1)}, bf16[128,128,128]{2,1,0:T(8,128)(2,1)}, u32[]{:S(2)}) copy-start(bf16[128,128,128]{2,1,0:T(8,128)(2,1)} %param.16) | copy-start | bytes 12582916
  20.1 35.9 %copy-start.2 = (f32[8,2048]{1,0:T(8,128)S(1)}, f32[8,2048]{1,0:T(8,128)}, u32[]{:S(2)}) copy-start(f32[8,2048]{1,0:T(8,128)} %param.13) | copy-start | bytes 196612
  20.2 14.7 %collective-permute-start.5 = (f32[8,6,128]{2,0,1:T(8,128)S(1)}, f32[8,6,128]{2,0,1:T(8,128)S(1)}, u32[]{:S(2)}, u32[]{:S(2)}) collective-permute-start(f32[8,6,128]{2,0,1:T(8,128)S(1)} %get-tuple-element.40), channel_id=1, source_target_pairs={{0,24},{8,32},{16,40},{24,48},{32,56},{40,64},{48,72},{56,80},{64,... | collective-permute-start | bytes 73736 | tf_op jit(solution)/shard_map/ppermute | solution.py:23
  26.2 8.7 %collective-permute-start.4 = (f32[8,6,128]{2,0,1:T(8,128)S(1)}, f32[8,6,128]{2,0,1:T(8,128)S(1)}, u32[]{:S(2)}, u32[]{:S(2)}) collective-permute-start(f32[8,6,128]{2,0,1:T(8,128)S(1)} %get-tuple-element.41), channel_id=1, source_target_pairs={{0,16},{8,24},{16,32},{24,40},{32,48},{40,56},{48,64},{56,72},{64,... | collective-permute-start | bytes 73736 | tf_op jit(solution)/shard_map/ppermute | solution.py:23
  29.5 5.3 %collective-permute-start.3 = (f32[8,6,128]{2,0,1:T(8,128)S(1)}, f32[8,6,128]{2,0,1:T(8,128)S(1)}, u32[]{:S(2)}, u32[]{:S(2)}) collective-permute-start(f32[8,6,128]{2,0,1:T(8,128)S(1)} %get-tuple-element.42), channel_id=1, source_target_pairs={{0,8},{8,16},{16,24},{24,32},{32,40},{40,48},{48,56},{56,64},{64,7... | collective-permute-start | bytes 73736 | tf_op jit(solution)/shard_map/ppermute | solution.py:23
